TPU v7x, 128 devices: a whole 4x4x4 slice. The times are simulated.
128 devices in a mesh: row: 4 (over x_hi, core), col: 32 (over y, x_lo, z).
Axes of the slice: x: 4 (x_hi: 2, x_lo: 2; x = x_hi * 2 + x_lo), y: 4, z: 4, core: 2. Of those that a mesh axis runs over, the one named last changes fastest.
Arguments:
- tokens: bfloat16 [49152, 2048], P('col', 'row'), may hold values from -6 to 6
- in_weight: float32 [2048, 6144], P(('row', 'col')), may hold values from -0.125 to 0.125
- out_weight: float32 [2048, 2048], P(('row', 'col')), may hold values from -0.125 to 0.125
- beta_weight: float32 [2048, 16], replicated, may hold values from -0.25 to 0.25
- conv_weight: float32 [4, 6144], P(None, 'row'), may hold values from -2.5 to 2.5
- conv_prior: bfloat16 [96, 3, 6144], P('col', None, 'row'), may hold values from -6 to 6
- head_gain: float32 [2048], P('row'), may hold values from 0.1 to 1.9
- state_pool: float32 [192, 16, 128, 128], P('col', 'row'), may hold values from -2.5 to 2.5
- state_index: int32 [96, 16], P('col', 'row'), may hold values from 0 to 5
- lengths: int32 [96], P('col'), may hold values from 1 to 512, 36864 in all
- page_table: int32 [96, 4, 2], P('col'), may hold values from 0 to 31, as said below
Outputs:
- server_in: bfloat16 [2048, 6144], P('row', 'col')
- server_out: bfloat16 [2048, 2048], P('row', 'col')
- layer_out: bfloat16 [49152, 2048], P('col', 'row')
- final_state: float32 [96, 16, 128, 128], P('col', 'row')
- page_cache: bfloat16 [384, 128, 2, 2048], P('col', None, None, 'row')
Inputs may be any that keep to these rules, and one draw needn't show every extreme that they name: `lengths`: one prompt has all 512 tokens live. `state_index`: which of its own index of col's 6 stored states a prompt and head continues. page_table[p, g, 0] is the index of col that keeps page g of prompt p and page_table[p, g, 1] its slot there, below 12; every slot of every index of col gets exactly one page; the prompts of one index of col send at most 1 pages to any one index of col, and exactly 1 to some.
All inputs are finite; a program needn't handle non-finite values. No bound on the sum of `lengths` on one device may be relied on, other than what follows from the above.
Results may differ from a plain program's by a relative error of at most 0.029.
Values may be sent and summed in bfloat16 or wider, within the bound.
No kernel may reach another device: no remote copies, remote signals or barrier semaphores. Data moves between devices by JAX's collectives and lax.ppermute only.
A program may use at most 128 MiB of HBM per device.

v0:
```python
import jax
import jax.numpy as jnp
from jax import lax
from jax.sharding import PartitionSpec as P

DK = 128
STRETCH = 64
CONV = 4
SEQ = 512
PAGE = 128
PAGES_SEQ = 4
HIGHEST = lax.Precision.HIGHEST


def delta_block(carry_state, block_data):
    query_unit, key_unit, values, beta_rates = block_data
    width_c = beta_rates.shape[1]
    width_k = key_unit.shape[2]
    strict_lower = jnp.tril(jnp.ones((width_c, width_c), jnp.float32), -1)
    causal = jnp.tril(jnp.ones((width_c, width_c), jnp.float32))
    gram_matrix = jnp.einsum("bik,bjk->bij", key_unit, key_unit, precision=HIGHEST)
    system = (
        jnp.eye(width_c, dtype=jnp.float32) + beta_rates[:, :, None] * gram_matrix * strict_lower
    )
    right_side = jnp.concatenate([key_unit, values], axis=2) * beta_rates[:, :, None]
    solved = jax.scipy.linalg.solve_triangular(system, right_side, lower=True, unit_diagonal=True)
    weighted = solved[:, :, :width_k]
    corrected = solved[:, :, width_k:] - jnp.einsum(
        "bck,bkv->bcv", weighted, carry_state, precision=HIGHEST
    )
    scores = jnp.einsum("bik,bjk->bij", query_unit, key_unit, precision=HIGHEST) * causal
    output = jnp.einsum("bck,bkv->bcv", query_unit, carry_state, precision=HIGHEST) + jnp.einsum(
        "bij,bjv->biv", scores, corrected, precision=HIGHEST
    )
    carry_state = carry_state + jnp.einsum("bck,bcv->bkv", key_unit, corrected, precision=HIGHEST)
    return (carry_state, output)


def delta_scan(query_unit, key_unit, values, beta_rates, initial, block_len):
    batch_n = query_unit.shape[0]
    length_all = query_unit.shape[1]
    num_blocks = length_all // block_len

    def to_blocks(tensor):
        shaped = tensor.reshape((batch_n, num_blocks, block_len) + tensor.shape[2:])
        return jnp.moveaxis(shaped, 1, 0)

    last_state, outputs = lax.scan(
        delta_block,
        initial,
        (to_blocks(query_unit), to_blocks(key_unit), to_blocks(values), to_blocks(beta_rates)),
    )
    outputs = jnp.moveaxis(outputs, 0, 1).reshape(batch_n, length_all, -1)
    return (last_state, outputs)


def unit_rows(tensor):
    return tensor * lax.rsqrt(jnp.sum(tensor * tensor, axis=-1, keepdims=True) + 1e-06)


def local(
    tokens,
    in_weight,
    out_weight,
    beta_weight,
    conv_weight,
    conv_prior,
    head_gain,
    state_pool,
    state_index,
    lengths,
    page_table,
):
    row_count = lax.axis_size("row")
    col_count = lax.axis_size("col")
    row_id = lax.axis_index("row")
    local_tokens = tokens.shape[0]
    feature_span = tokens.shape[1]
    head_group = state_index.shape[1]
    head_width = 3 * DK
    prompts_here = lengths.shape[0]
    trainer_in = in_weight.astype(jnp.bfloat16)
    server_in, server_out = (
        lax.all_to_all(trainer_in, "col", split_axis=1, concat_axis=0, tiled=True),
        lax.all_to_all(
            out_weight.astype(jnp.bfloat16), "col", split_axis=1, concat_axis=0, tiled=True
        ),
    )
    beta_cast = beta_weight.astype(jnp.bfloat16)
    wide_in, wide_out = (
        lax.all_gather(server_in, "col", axis=1, tiled=True),
        lax.all_gather(server_out, "col", axis=1, tiled=True),
    )
    columns = wide_in
    product = jnp.dot(tokens, columns, preferred_element_type=jnp.float32)
    qkv_sum = lax.psum_scatter(
        product.reshape(local_tokens, lax.axis_size("row") * head_group, head_width)
        .transpose(1, 0, 2)
        .astype(jnp.bfloat16),
        "row",
        scatter_dimension=0,
        tiled=True,
    )
    beta_rows = lax.dynamic_slice_in_dim(beta_cast, row_id * feature_span, feature_span, 0)
    beta_term = jnp.dot(tokens, beta_rows, preferred_element_type=jnp.float32).T
    beta_sum = lax.psum_scatter(
        beta_term.astype(jnp.bfloat16), "row", scatter_dimension=0, tiled=True
    ).astype(jnp.float32)
    projected = qkv_sum.reshape(head_group, prompts_here, SEQ, head_width)
    prior_rows = conv_prior.reshape(prompts_here, CONV - 1, head_group, head_width).transpose(
        2, 0, 1, 3
    )
    padded = jnp.concatenate(
        [prior_rows.astype(jnp.float32), projected.astype(jnp.float32)], axis=2
    )
    taps_all = conv_weight.reshape(CONV, head_group, head_width)
    conv_sum = jnp.zeros(projected.shape, jnp.float32)
    for tap_id in range(CONV):
        conv_sum = (
            conv_sum + taps_all[tap_id][:, None, None, :] * padded[:, :, tap_id : tap_id + SEQ]
        )
    activated = jax.nn.silu(conv_sum).reshape(head_group * prompts_here, SEQ, 3, DK)
    query_unit = unit_rows(activated[:, :, 0])
    key_unit = unit_rows(activated[:, :, 1])
    values = activated[:, :, 2]
    live_mask = (jnp.arange(SEQ, dtype=jnp.int32)[None, :] < lengths[:, None]).astype(jnp.float32)
    live_batch = jnp.broadcast_to(live_mask[None], (head_group, prompts_here, SEQ)).reshape(
        head_group * prompts_here, SEQ
    )
    beta_rates = live_batch * jax.nn.sigmoid(beta_sum.reshape(head_group * prompts_here, SEQ))
    picked = state_pool[state_index, jnp.arange(head_group, dtype=jnp.int32)[None, :]]
    initial = picked.transpose(1, 0, 2, 3).reshape(head_group * prompts_here, DK, DK)
    last_state, outputs = delta_scan(query_unit, key_unit, values, beta_rates, initial, STRETCH)
    outputs = outputs * live_batch[:, :, None]
    normed = outputs.reshape(head_group, prompts_here, SEQ, DK)
    normed = (
        normed
        * lax.rsqrt(jnp.mean(normed * normed, axis=3, keepdims=True) + 1e-05)
        * head_gain.reshape(head_group, 1, 1, DK)
    )
    flat_heads = (
        normed.astype(jnp.bfloat16).transpose(1, 2, 0, 3).reshape(local_tokens, head_group * DK)
    )
    out_span = wide_out.shape[1] // row_count
    columns = wide_out
    product = jnp.dot(flat_heads, columns, preferred_element_type=jnp.float32)
    layer_out = (
        lax.psum_scatter(
            product.reshape(local_tokens, lax.axis_size("row") * 1, out_span)
            .transpose(1, 0, 2)
            .astype(jnp.bfloat16),
            "row",
            scatter_dimension=0,
            tiled=True,
        )
        .astype(jnp.float32)[0]
        .astype(jnp.bfloat16)
    )
    final_state = last_state.reshape(head_group, prompts_here, DK, DK).transpose(1, 0, 2, 3)
    keep_mask = live_batch[:, :, None]
    kept_pairs = jnp.stack([key_unit * keep_mask, values * keep_mask], axis=0).reshape(
        2, head_group, prompts_here, SEQ, DK
    )
    page_rows = (
        kept_pairs.transpose(2, 3, 0, 1, 4)
        .reshape(prompts_here * PAGES_SEQ, PAGE, 2, head_group * DK)
        .astype(jnp.bfloat16)
    )
    pages_dev = page_rows.shape[0]
    capacity = max(1, 2 * pages_dev // col_count)
    targets = page_table[:, :, 0].reshape(-1)
    slot_ids = page_table[:, :, 1].reshape(-1)
    order_ids = jnp.arange(pages_dev, dtype=jnp.int32)
    earlier = (targets[:, None] == targets[None, :]) & (order_ids[None, :] < order_ids[:, None])
    positions = targets * capacity + jnp.sum(earlier.astype(jnp.int32), axis=1)
    outgoing = (
        jnp.zeros((col_count * capacity,) + page_rows.shape[1:], jnp.bfloat16)
        .at[positions]
        .set(page_rows)
    )
    slot_send = jnp.full((col_count * capacity,), pages_dev, jnp.int32).at[positions].set(slot_ids)
    arrived, arrived_slots = (
        lax.all_to_all(outgoing, "col", split_axis=0, concat_axis=0, tiled=True),
        lax.all_to_all(slot_send, "col", split_axis=0, concat_axis=0, tiled=True),
    )
    page_cache = (
        jnp.zeros(page_rows.shape, jnp.bfloat16).at[arrived_slots].set(arrived, mode="drop")
    )
    return (server_in, server_out, layer_out, final_state, page_cache)


def solution(mesh):
    return jax.shard_map(
        local,
        mesh=mesh,
        in_specs=(
            P("col", "row"),
            P(("row", "col"), None),
            P(("row", "col"), None),
            P(),
            P(None, "row"),
            P("col", None, "row"),
            P("row"),
            P("col", "row", None, None),
            P("col", "row"),
            P("col"),
            P("col", None, None),
        ),
        out_specs=(
            P("row", "col"),
            P("row", "col"),
            P("col", "row"),
            P("col", "row", None, None),
            P("col", None, None, "row"),
        ),
        check_vma=False,
    )
```

profile of v0, /device:TPU:16, one launch (start us, length us, event | category | flops | bytes accessed | tf_op | source)
XLA Modules:
  0.0 1226.2 jit_solution(3627169898886624098)
XLA Ops:
  8.8 16.4 %all_to_all.55 = bf16[16,32,192]{2,0,1:T(8,128)(2,1)S(1)} all-to-all(bf16[16,32,192]{2,0,1:T(8,128)(2,1)S(1)} %copy.123), channel_id=1, replica_groups=mesh['row'=4,'col'=32] {'col'}, dimensions={1} | all-to-all | bytes 393216 | tf_op jit(solution)/shard_map/all_to_all | solution.py:84
  26.1 144.7 %all-gather.3.cloned.1.call-done = bf16[512,6144]{0,1:T(8,128)(2,1)} async-done(((bf16[512,192]{0,1:T(8,128)(2,1)}), bf16[512,6144]{0,1:T(8,128)(2,1)}) %all-gather.3.cloned.1.call-update) | async-done | bytes 6291472 | tf_op jit(solution)/shard_map/all_gather | solution.py:91
  170.8 15.9 %convolution_convert_fusion = bf16[1536,6144]{1,0:T(8,128)(2,1)} fusion(bf16[1536,512]{1,0:T(8,128)(2,1)S(1)} %copy-done, bf16[512,6144]{0,1:T(8,128)(2,1)} %all-gather.3.cloned.1.call-done), kind=kOutput, calls=%fused_computation.43 | convolution fusion | flops 9673113600 | bytes 26738688 | tf_op jit(solution)/shard_map/dot_general | solution.py:95
  186.7 18.3 %copy.164 = bf16[192,16,8,384]{3,2,0,1:T(8,128)(2,1)} copy(bf16[192,16,8,384]{3,2,1,0:T(8,128)(2,1)} %bitcast.161) | data formatting | bytes 37748736 | tf_op jit(solution)/shard_map/convert_element_type | solution.py:99
  207.0 25.2 %all-to-all-start.1 = ((bf16[32,2,512]{2,1,0:T(2,128)(2,1)}), bf16[32,2,512]{2,1,0:T(2,128)(2,1)S(1)}, u32[]{:S(2)}, u32[]{:S(2)}) async-start(bf16[32,2,512]{2,1,0:T(2,128)(2,1)} %reshape.338), calls=%async_computation.1 | async-start | bytes 131072 | tf_op jit(solution)/shard_map/all_to_all | solution.py:85
  234.8 13.6 %all-reduce = bf16[16,1536]{1,0:T(8,128)(2,1)S(1)} all-reduce(bf16[16,1536]{1,0:T(8,128)(2,1)S(1)} %convolution_convert_fusion.1), channel_id=3, replica_groups=mesh['row'=4,'col'=32] {'row'}, use_global_device_ids=true, to_apply=%region_3.4.clone | all-reduce | flops 24576 | bytes 98304
  249.1 2.4 gather_fusion
  252.5 116.9 %reduce-scatter.3.cloned.1.call-done = bf16[4,1536,384]{2,1,0:T(8,128)(2,1)} async-done(((bf16[16,1536,384]{2,1,0:T(8,128)(2,1)}), bf16[4,1536,384]{2,1,0:T(8,128)(2,1)}) %reduce-scatter.3.cloned.1.call-update) | async-done | bytes 4718608 | tf_op jit(solution)/shard_map/reduce_scatter | solution.py:96
  369.3 3.2 convert.14
  372.6 7.4 divide_multiply_fusion
  380.0 9.7 copy.129
  389.6 8.1 multiply_reduce_fusion
  397.8 3.5 copy.130
  401.4 3.6 copy.132
  405.0 3.6 copy.131
  408.6 3.8 multiply_bitcast_fusion.1
  412.4 2.1 multiply_bitcast_fusion
  414.5 554.7 %while.12 = (s32[]{:T(128)}, f32[12,128,128]{2,1,0:T(8,128)S(1)}, f32[8,12,64,128]{3,2,0,1:T(8,128)}, f32[8,12,64,128]{3,2,0,1:T(8,128)}, f32[8,12,64]{2,0,1:T(8...) while((s32[]{:T(128)}, f32[12,128,128]{2,1,0:T(8,128)S(1)}, ...), condition=%wide.region_5.6_spmd, body=%wide.region_4.5_spmd.sunk | while | flops 831590464 | bytes 12349789 | solution.py:48
  416.7 59.0 %custom-call.8 = f32[12,1,64,64]{2,3,1,0:T(8,128)S(1)} custom-call(f32[12,1,64,64]{3,2,1,0:T(8,128)S(1)} %fusion.93), custom_call_target="InvertDiagBlocksLowerTriangular" | custom-call | tf_op jit(solution)/shard_map/while/body/eval_jaxpr/jit(_solve_triangular)/vmap()/triangular_solve | solution.py:26
  477.5 1.8 convolution_multiply_fusion.3
  479.8 2.6 fusion.97
  486.0 59.0 %custom-call.8 = f32[12,1,64,64]{2,3,1,0:T(8,128)S(1)} custom-call(f32[12,1,64,64]{3,2,1,0:T(8,128)S(1)} %fusion.93), custom_call_target="InvertDiagBlocksLowerTriangular" | custom-call | tf_op jit(solution)/shard_map/while/body/eval_jaxpr/jit(_solve_triangular)/vmap()/triangular_solve | solution.py:26
  546.9 1.8 convolution_multiply_fusion.3
  549.1 2.6 fusion.97
  551.7 1.4 convolution_add_fusion.3
  555.4 59.0 %custom-call.8 = f32[12,1,64,64]{2,3,1,0:T(8,128)S(1)} custom-call(f32[12,1,64,64]{3,2,1,0:T(8,128)S(1)} %fusion.93), custom_call_target="InvertDiagBlocksLowerTriangular" | custom-call | tf_op jit(solution)/shard_map/while/body/eval_jaxpr/jit(_solve_triangular)/vmap()/triangular_solve | solution.py:26
  616.2 1.8 convolution_multiply_fusion.3
  618.5 2.6 fusion.97
  624.7 59.0 %custom-call.8 = f32[12,1,64,64]{2,3,1,0:T(8,128)S(1)} custom-call(f32[12,1,64,64]{3,2,1,0:T(8,128)S(1)} %fusion.93), custom_call_target="InvertDiagBlocksLowerTriangular" | custom-call | tf_op jit(solution)/shard_map/while/body/eval_jaxpr/jit(_solve_triangular)/vmap()/triangular_solve | solution.py:26
  685.5 1.8 convolution_multiply_fusion.3
  687.8 2.6 fusion.97
  690.4 1.4 convolution_add_fusion.3
  694.0 59.0 %custom-call.8 = f32[12,1,64,64]{2,3,1,0:T(8,128)S(1)} custom-call(f32[12,1,64,64]{3,2,1,0:T(8,128)S(1)} %fusion.93), custom_call_target="InvertDiagBlocksLowerTriangular" | custom-call | tf_op jit(solution)/shard_map/while/body/eval_jaxpr/jit(_solve_triangular)/vmap()/triangular_solve | solution.py:26
  754.9 1.7 convolution_multiply_fusion.3
  757.1 2.6 fusion.97
  759.7 1.4 convolution_add_fusion.3
  763.4 59.0 %custom-call.8 = f32[12,1,64,64]{2,3,1,0:T(8,128)S(1)} custom-call(f32[12,1,64,64]{3,2,1,0:T(8,128)S(1)} %fusion.93), custom_call_target="InvertDiagBlocksLowerTriangular" | custom-call | tf_op jit(solution)/shard_map/while/body/eval_jaxpr/jit(_solve_triangular)/vmap()/triangular_solve | solution.py:26
  824.2 1.8 convolution_multiply_fusion.3
  826.5 2.6 fusion.97
  832.7 59.0 %custom-call.8 = f32[12,1,64,64]{2,3,1,0:T(8,128)S(1)} custom-call(f32[12,1,64,64]{3,2,1,0:T(8,128)S(1)} %fusion.93), custom_call_target="InvertDiagBlocksLowerTriangular" | custom-call | tf_op jit(solution)/shard_map/while/body/eval_jaxpr/jit(_solve_triangular)/vmap()/triangular_solve | solution.py:26
  893.5 1.8 convolution_multiply_fusion.3
  895.8 2.6 fusion.97
  898.4 1.4 convolution_add_fusion.3
  902.0 59.0 %custom-call.8 = f32[12,1,64,64]{2,3,1,0:T(8,128)S(1)} custom-call(f32[12,1,64,64]{3,2,1,0:T(8,128)S(1)} %fusion.93), custom_call_target="InvertDiagBlocksLowerTriangular" | custom-call | tf_op jit(solution)/shard_map/while/body/eval_jaxpr/jit(_solve_triangular)/vmap()/triangular_solve | solution.py:26
  962.9 1.8 convolution_multiply_fusion.3
  965.1 2.6 fusion.97
  969.2 3.4 fusion.32
  972.8 2.6 fusion.33
  976.6 2.0 reshape.325
  978.6 8.2 convert_bitcast_fusion
  989.3 7.6 all-to-all-start.2
  997.2 5.3 copy.142
  1002.5 4.9 copy.143
  1007.4 9.9 multiply_convert_fusion.1
  1017.4 3.9 maximum_bitcast_fusion
  1021.3 5.7 reshape.308
  1027.1 3.9 copy.144
  1030.9 4.2 broadcast_in_dim.32
  1035.1 8.4 scatter_fusion
  1043.5 8.3 all-to-all-start.3
  1053.5 139.6 %all-to-all-done.3 = bf16[32,128,2,512]{3,1,2,0:T(8,128)(2,1)} async-done(((bf16[32,128,2,512]{3,1,2,0:T(8,128)(2,1)}), bf16[32,128,2,512]{3,1,2,0:T(8,128)(2,1)}, u32[]{:S(2)}, u32[]{:S(2)}) %all-to-all-start.3) | async-done | bytes 8388640 | tf_op jit(solution)/shard_map/all_to_all | solution.py:183
  1193.1 2.1 broadcast_in_dim.25
  1195.2 17.7 %scatter_fusion.1 = bf16[12,128,2,512]{3,1,2,0:T(8,128)(2,1)} fusion(bf16[12,128,2,512]{3,1,2,0:T(8,128)(2,1)} %broadcast_in_dim.25, s32[32]{0:T(128)S(1)} %fusion.41, bf16[32,128,2,512]{3,1,2,0:T(8,128)(2,1)} %all-to-all-done.3), kind=kCustom, calls=%fused_computation.3 | custom fusion | bytes 25165952 | tf_op jit(solution)/shard_map/scatter | solution.py:187
  1212.8 6.8 copy.148
  (182 shorter events, 55.2 us)
Async XLA Ops:
  7.2 163.6 %copy-start = (bf16[1536,512]{1,0:T(8,128)(2,1)S(1)}, bf16[1536,512]{1,0:T(8,128)(2,1)}, u32[]{:S(2)}) copy-start(bf16[1536,512]{1,0:T(8,128)(2,1)} %param.13) | copy-start | bytes 4718596
  7.2 163.6 %all-gather.3.cloned.1.call-start = ((), (), s32[]{:S(2)}) async-start(), calls=%async_computation.6 | async-start | bytes 6488064 | tf_op jit(solution)/shard_map/all_gather | solution.py:91
  26.1 343.3 %reduce-scatter.3.cloned.1.call-start = ((), (), s32[]{:S(2)}) async-start(), calls=%async_computation.7 | async-start | bytes 23592960 | tf_op jit(solution)/shard_map/reduce_scatter | solution.py:96
  205.0 0.9 copy-start.3
  205.0 27.3 %copy-start.10 = (u32[128]{0:T(128)S(1)}, u32[128]{0:T(128)}, u32[]{:S(2)}) copy-start(u32[128]{0:T(128)} %constant.92) | copy-start | bytes 1540
  205.0 43.5 %copy-start.9 = (s32[3]{0:T(128)S(1)}, s32[3]{0:T(128)}, u32[]{:S(2)}) copy-start(s32[3]{0:T(128)} %param.22) | copy-start | bytes 40
  205.0 43.7 %copy-start.8 = (s32[3,4]{1,0:T(4,128)S(1)}, s32[3,4]{1,0:T(4,128)}, u32[]{:S(2)}) copy-start(s32[3,4]{1,0:T(4,128)} %param.21) | copy-start | bytes 148
  205.9 42.9 %copy-start.5 = (f32[4,1536]{1,0:T(4,128)S(1)}, f32[4,1536]{1,0:T(4,128)}, u32[]{:S(2)}) copy-start(f32[4,1536]{1,0:T(4,128)} %param.17) | copy-start | bytes 73732
  205.9 43.0 %copy-start.4 = (bf16[3,3,1536]{2,1,0:T(4,128)(2,1)S(1)}, bf16[3,3,1536]{2,1,0:T(4,128)(2,1)}, u32[]{:S(2)}) copy-start(bf16[3,3,1536]{2,1,0:T(4,128)(2,1)} %param.18) | copy-start | bytes 82948
  207.0 44.6 %all-to-all-start.1 = ((bf16[32,2,512]{2,1,0:T(2,128)(2,1)}), bf16[32,2,512]{2,1,0:T(2,128)(2,1)S(1)}, u32[]{:S(2)}, u32[]{:S(2)}) async-start(bf16[32,2,512]{2,1,0:T(2,128)(2,1)} %reshape.338), calls=%async_computation.1 | async-start | bytes 131072 | tf_op jit(solution)/shard_map/all_to_all | solution.py:85
  232.2 746.4 %all-gather.5.cloned.1.call-start = ((), (), s32[]{:S(2)}) async-start(), calls=%async_computation.8 | async-start | bytes 2162688 | tf_op jit(solution)/shard_map/all_gather | solution.py:92
  252.4 967.2 %reduce-scatter.5.cloned.1.call-start = ((), (), s32[]{:S(2)}) async-start(), calls=%async_computation.9 | async-start | bytes 7864320 | tf_op jit(solution)/shard_map/reduce_scatter | solution.py:148
  408.6 3.8 copy-start.2
  969.2 3.6 copy-start.7
  986.8 0.7 copy-start.6
  989.3 54.2 %all-to-all-start.2 = ((s32[32,1,1]{2,1,0:T(1,128)}), s32[32,1,1]{2,1,0:T(1,128)S(1)}, u32[]{:S(2)}, u32[]{:S(2)}) async-start(s32[32,1,1]{2,1,0:T(1,128)} %copy.140), calls=%async_computation.4 | async-start | bytes 32768 | tf_op jit(solution)/shard_map/all_to_all | solution.py:184
  1043.5 149.6 %all-to-all-start.3 = ((bf16[32,128,2,512]{3,1,2,0:T(8,128)(2,1)}), bf16[32,128,2,512]{3,1,2,0:T(8,128)(2,1)}, u32[]{:S(2)}, u32[]{:S(2)}) async-start(bf16[32,128,2,512]{3,1,2,0:T(8,128)(2,1)} %scatter_fusion), calls=%async_computation.5 | async-start | bytes 16777216 | tf_op jit(solution)/shard_map/all_to_all | solution.py:183
  1195.2 24.5 %copy-start.1 = (bf16[1536,512]{1,0:T(8,128)(2,1)S(1)}, bf16[1536,512]{1,0:T(8,128)(2,1)}, u32[]{:S(2)}) copy-start(bf16[1536,512]{1,0:T(8,128)(2,1)} %param.13) | copy-start | bytes 4718596
Sparse Core Ops, SparseCore 0:
  26.2 144.5 all-gather.2
  205.2 164.0 reduce-scatter.2
  371.7 135.9 all-gather.4
  987.0 64.7 reduce-scatter.4
where the time goes:
time: 1230 us
  other arithmetic  520 us (42%)
  waiting for transfers between devices  401 us (33%)
  local copies, waits for them, and re-layouts  122 us (10%)
  matrix products  96.3 us (8%)
  starting transfers between devices  41.4 us (3%)
  blocking collectives  30 us (2%)
  between operations  14.8 us (1%)
    another operation x32, other arithmetic, delta_block(): jax.scipy.linalg.solve_triangular(system, right_side, lower=True, unit_di...  473 us
    all_gather x1, waiting for transfers between devices, local(): lax.all_gather(server_in, 'col', axis=1, tiled=True)  145 us
    all_to_all x1, waiting for transfers between devices, local(): lax.all_to_all(outgoing, 'col', split_axis=0, concat_axis=0, tiled=True)  140 us
    reduce_scatter x1, waiting for transfers between devices, local(): lax.psum_scatter(product.reshape(local_tokens, lax.axis_size('row') * hea...  117 us
    all_to_all x1, starting transfers between devices, local(): lax.all_to_all(out_weight.astype(jnp.bfloat16), 'col', split_axis=1, conc...  25.2 us
  transfers between devices with their start and end apart: 7, of which 3 were waited for; matrix products, arithmetic and copies ran while one was open for 56% of the time, Pallas kernels for 0%

commit v1 on v0

--- a/solution.py
+++ b/solution.py
@@ -82,8 +82,14 @@
     trainer_in = in_weight.astype(jnp.bfloat16)
     server_in, server_out = (
         lax.all_to_all(trainer_in, "col", split_axis=1, concat_axis=0, tiled=True),
-        lax.all_to_all(
-            out_weight.astype(jnp.bfloat16), "col", split_axis=1, concat_axis=0, tiled=True
+        jnp.concatenate(
+            lax.all_to_all(
+                jnp.stack(jnp.split(out_weight.astype(jnp.bfloat16), lax.axis_size("col"), axis=1)),
+                "col",
+                0,
+                0,
+            ),
+            axis=0,
         ),
     )
     beta_cast = beta_weight.astype(jnp.bfloat16)

time: 1230 us -> 1230 us (level)
  no operation moved by 1% of the time
where the time goes in v1:
time: 1230 us
  other arithmetic  520 us (42%)
  waiting for transfers between devices  400 us (33%)
  local copies, waits for them, and re-layouts  123 us (10%)
  matrix products  96.3 us (8%)
  starting transfers between devices  41.4 us (3%)
  blocking collectives  30 us (2%)
  between operations  14.8 us (1%)
    another operation x32, other arithmetic, delta_block(): jax.scipy.linalg.solve_triangular(system, right_side, lower=True, unit_di...  473 us
    all_gather x1, waiting for transfers between devices, local(): lax.all_gather(server_in, 'col', axis=1, tiled=True)  145 us
    all_to_all x1, waiting for transfers between devices, local(): lax.all_to_all(outgoing, 'col', split_axis=0, concat_axis=0, tiled=True)  140 us
    reduce_scatter x1, waiting for transfers between devices, local(): lax.psum_scatter(product.reshape(local_tokens, lax.axis_size('row') * hea...  116 us
    all_to_all x1, starting transfers between devices, local(): lax.all_to_all(jnp.stack(jnp.split(out_weight.astype(jnp.bfloat16), lax.a...  25.2 us
  transfers between devices with their start and end apart: 7, of which 3 were waited for; matrix products, arithmetic and copies ran while one was open for 56% of the time, Pallas kernels for 0%

profile of v1, /device:TPU:16, one launch (start us, length us, event | category | flops | bytes accessed | tf_op | source)
XLA Modules:
  0.0 1226.2 jit_solution(13301100050469628550)
XLA Ops:
  8.8 16.4 %all_to_all.41 = bf16[16,32,192]{2,0,1:T(8,128)(2,1)S(1)} all-to-all(bf16[16,32,192]{2,0,1:T(8,128)(2,1)S(1)} %copy.119), channel_id=1, replica_groups=mesh['row'=4,'col'=32] {'col'}, dimensions={1} | all-to-all | bytes 393216 | tf_op jit(solution)/shard_map/all_to_all | solution.py:84
  26.1 144.7 %all-gather.3.cloned.1.call-done = bf16[512,6144]{0,1:T(8,128)(2,1)} async-done(((bf16[512,192]{0,1:T(8,128)(2,1)}), bf16[512,6144]{0,1:T(8,128)(2,1)}) %all-gather.3.cloned.1.call-update) | async-done | bytes 6291472 | tf_op jit(solution)/shard_map/all_gather | solution.py:97
  170.8 15.9 %convolution_convert_fusion = bf16[1536,6144]{1,0:T(8,128)(2,1)} fusion(bf16[1536,512]{1,0:T(8,128)(2,1)S(1)} %copy-done, bf16[512,6144]{0,1:T(8,128)(2,1)} %all-gather.3.cloned.1.call-done), kind=kOutput, calls=%fused_computation.43 | convolution fusion | flops 9673113600 | bytes 26738688 | tf_op jit(solution)/shard_map/dot_general | solution.py:101
  186.7 18.3 %copy.158 = bf16[192,16,8,384]{3,2,0,1:T(8,128)(2,1)} copy(bf16[192,16,8,384]{3,2,1,0:T(8,128)(2,1)} %bitcast.283) | data formatting | bytes 37748736 | tf_op jit(solution)/shard_map/convert_element_type | solution.py:105
  208.2 25.2 %all-to-all-start.1 = ((bf16[32,2,512]{2,1,0:T(2,128)(2,1)}), bf16[32,2,512]{2,1,0:T(2,128)(2,1)S(1)}, u32[]{:S(2)}, u32[]{:S(2)}) async-start(bf16[32,2,512]{2,1,0:T(2,128)(2,1)} %reshape.339), calls=%async_computation.1 | async-start | bytes 131072 | tf_op jit(solution)/shard_map/all_to_all | solution.py:86
  236.0 13.6 %all-reduce = bf16[16,1536]{1,0:T(8,128)(2,1)S(1)} all-reduce(bf16[16,1536]{1,0:T(8,128)(2,1)S(1)} %convolution_convert_fusion.1), channel_id=3, replica_groups=mesh['row'=4,'col'=32] {'row'}, use_global_device_ids=true, to_apply=%region_3.4.clone | all-reduce | flops 24576 | bytes 98304
  250.3 2.3 gather_fusion
  253.6 115.7 %reduce-scatter.3.cloned.1.call-done = bf16[4,1536,384]{2,1,0:T(8,128)(2,1)} async-done(((bf16[16,1536,384]{2,1,0:T(8,128)(2,1)}), bf16[4,1536,384]{2,1,0:T(8,128)(2,1)}) %reduce-scatter.3.cloned.1.call-update) | async-done | bytes 4718608 | tf_op jit(solution)/shard_map/reduce_scatter | solution.py:102
  369.4 3.2 convert.14
  372.6 7.4 divide_multiply_fusion
  380.0 9.7 copy.124
  389.7 8.1 multiply_reduce_fusion
  397.8 3.5 copy.125
  401.5 3.6 copy.127
  405.0 3.6 copy.126
  408.6 3.8 multiply_bitcast_fusion.1
  412.4 2.1 multiply_bitcast_fusion
  414.5 554.7 %while.12 = (s32[]{:T(128)}, f32[12,128,128]{2,1,0:T(8,128)S(1)}, f32[8,12,64,128]{3,2,0,1:T(8,128)}, f32[8,12,64,128]{3,2,0,1:T(8,128)}, f32[8,12,64]{2,0,1:T(8...) while((s32[]{:T(128)}, f32[12,128,128]{2,1,0:T(8,128)S(1)}, ...), condition=%wide.region_5.6_spmd, body=%wide.region_4.5_spmd.sunk | while | flops 831590464 | bytes 12349789 | solution.py:48
  416.7 59.0 %custom-call.10 = f32[12,1,64,64]{2,3,1,0:T(8,128)S(1)} custom-call(f32[12,1,64,64]{3,2,1,0:T(8,128)S(1)} %fusion.93), custom_call_target="InvertDiagBlocksLowerTriangular" | custom-call | tf_op jit(solution)/shard_map/while/body/eval_jaxpr/jit(_solve_triangular)/vmap()/triangular_solve | solution.py:26
  477.5 1.8 convolution_multiply_fusion.3
  479.8 2.6 fusion.97
  486.0 59.0 %custom-call.10 = f32[12,1,64,64]{2,3,1,0:T(8,128)S(1)} custom-call(f32[12,1,64,64]{3,2,1,0:T(8,128)S(1)} %fusion.93), custom_call_target="InvertDiagBlocksLowerTriangular" | custom-call | tf_op jit(solution)/shard_map/while/body/eval_jaxpr/jit(_solve_triangular)/vmap()/triangular_solve | solution.py:26
  546.9 1.8 convolution_multiply_fusion.3
  549.2 2.6 fusion.97
  551.7 1.4 convolution_add_fusion.3
  555.4 59.0 %custom-call.10 = f32[12,1,64,64]{2,3,1,0:T(8,128)S(1)} custom-call(f32[12,1,64,64]{3,2,1,0:T(8,128)S(1)} %fusion.93), custom_call_target="InvertDiagBlocksLowerTriangular" | custom-call | tf_op jit(solution)/shard_map/while/body/eval_jaxpr/jit(_solve_triangular)/vmap()/triangular_solve | solution.py:26
  616.2 1.7 convolution_multiply_fusion.3
  618.5 2.6 fusion.97
  621.1 1.4 convolution_add_fusion.3
  624.7 59.0 %custom-call.10 = f32[12,1,64,64]{2,3,1,0:T(8,128)S(1)} custom-call(f32[12,1,64,64]{3,2,1,0:T(8,128)S(1)} %fusion.93), custom_call_target="InvertDiagBlocksLowerTriangular" | custom-call | tf_op jit(solution)/shard_map/while/body/eval_jaxpr/jit(_solve_triangular)/vmap()/triangular_solve | solution.py:26
  685.6 1.8 convolution_multiply_fusion.3
  687.8 2.6 fusion.97
  694.0 59.0 %custom-call.10 = f32[12,1,64,64]{2,3,1,0:T(8,128)S(1)} custom-call(f32[12,1,64,64]{3,2,1,0:T(8,128)S(1)} %fusion.93), custom_call_target="InvertDiagBlocksLowerTriangular" | custom-call | tf_op jit(solution)/shard_map/while/body/eval_jaxpr/jit(_solve_triangular)/vmap()/triangular_solve | solution.py:26
  754.9 1.8 convolution_multiply_fusion.3
  757.2 2.6 fusion.97
  759.7 1.4 convolution_add_fusion.3
  763.4 59.0 %custom-call.10 = f32[12,1,64,64]{2,3,1,0:T(8,128)S(1)} custom-call(f32[12,1,64,64]{3,2,1,0:T(8,128)S(1)} %fusion.93), custom_call_target="InvertDiagBlocksLowerTriangular" | custom-call | tf_op jit(solution)/shard_map/while/body/eval_jaxpr/jit(_solve_triangular)/vmap()/triangular_solve | solution.py:26
  824.2 1.8 convolution_multiply_fusion.3
  826.5 2.6 fusion.97
  832.7 59.0 %custom-call.10 = f32[12,1,64,64]{2,3,1,0:T(8,128)S(1)} custom-call(f32[12,1,64,64]{3,2,1,0:T(8,128)S(1)} %fusion.93), custom_call_target="InvertDiagBlocksLowerTriangular" | custom-call | tf_op jit(solution)/shard_map/while/body/eval_jaxpr/jit(_solve_triangular)/vmap()/triangular_solve | solution.py:26
  893.6 1.8 convolution_multiply_fusion.3
  895.8 2.6 fusion.97
  898.4 1.4 convolution_add_fusion.3
  902.0 59.0 %custom-call.10 = f32[12,1,64,64]{2,3,1,0:T(8,128)S(1)} custom-call(f32[12,1,64,64]{3,2,1,0:T(8,128)S(1)} %fusion.93), custom_call_target="InvertDiagBlocksLowerTriangular" | custom-call | tf_op jit(solution)/shard_map/while/body/eval_jaxpr/jit(_solve_triangular)/vmap()/triangular_solve | solution.py:26
  962.9 1.7 convolution_multiply_fusion.3
  965.2 2.6 fusion.97
  969.2 3.4 fusion.32
  972.8 2.6 fusion.33
  976.6 2.0 reshape.326
  978.6 8.2 convert_bitcast_fusion
  989.3 7.6 all-to-all-start.2
  997.3 5.2 copy.137
  1002.5 4.9 copy.138
  1007.4 10.0 multiply_convert_fusion.1
  1017.4 3.9 maximum_bitcast_fusion
  1021.3 5.7 reshape.309
  1027.1 3.9 copy.139
  1030.9 4.2 broadcast_in_dim.32
  1035.1 8.4 scatter_fusion
  1043.5 8.4 all-to-all-start.3
  1053.5 139.6 %all-to-all-done.3 = bf16[32,128,2,512]{3,1,2,0:T(8,128)(2,1)} async-done(((bf16[32,128,2,512]{3,1,2,0:T(8,128)(2,1)}), bf16[32,128,2,512]{3,1,2,0:T(8,128)(2,1)}, u32[]{:S(2)}, u32[]{:S(2)}) %all-to-all-start.3) | async-done | bytes 8388640 | tf_op jit(solution)/shard_map/all_to_all | solution.py:189
  1193.1 2.1 broadcast_in_dim.25
  1195.2 17.7 %scatter_fusion.1 = bf16[12,128,2,512]{3,1,2,0:T(8,128)(2,1)} fusion(bf16[12,128,2,512]{3,1,2,0:T(8,128)(2,1)} %broadcast_in_dim.25, s32[32]{0:T(128)S(1)} %fusion.41, bf16[32,128,2,512]{3,1,2,0:T(8,128)(2,1)} %all-to-all-done.3), kind=kCustom, calls=%fused_computation.3 | custom fusion | bytes 25165952 | tf_op jit(solution)/shard_map/scatter | solution.py:193
  1212.9 6.8 copy.143
  (212 shorter events, 56.4 us)
Async XLA Ops:
  7.2 163.6 %copy-start = (bf16[1536,512]{1,0:T(8,128)(2,1)S(1)}, bf16[1536,512]{1,0:T(8,128)(2,1)}, u32[]{:S(2)}) copy-start(bf16[1536,512]{1,0:T(8,128)(2,1)} %param.13) | copy-start | bytes 4718596
  7.2 163.6 %all-gather.3.cloned.1.call-start = ((), (), s32[]{:S(2)}) async-start(), calls=%async_computation.6 | async-start | bytes 6488064 | tf_op jit(solution)/shard_map/all_gather | solution.py:97
  26.1 343.3 %reduce-scatter.3.cloned.1.call-start = ((), (), s32[]{:S(2)}) async-start(), calls=%async_computation.7 | async-start | bytes 23592960 | tf_op jit(solution)/shard_map/reduce_scatter | solution.py:102
  205.0 0.9 copy-start.3
  205.0 28.5 %copy-start.10 = (u32[128]{0:T(128)S(1)}, u32[128]{0:T(128)}, u32[]{:S(2)}) copy-start(u32[128]{0:T(128)} %constant.92) | copy-start | bytes 1540
  205.0 44.8 %copy-start.9 = (s32[3]{0:T(128)S(1)}, s32[3]{0:T(128)}, u32[]{:S(2)}) copy-start(s32[3]{0:T(128)} %param.22) | copy-start | bytes 40
  205.0 44.9 %copy-start.8 = (s32[3,4]{1,0:T(4,128)S(1)}, s32[3,4]{1,0:T(4,128)}, u32[]{:S(2)}) copy-start(s32[3,4]{1,0:T(4,128)} %param.21) | copy-start | bytes 148
  205.0 44.9 %copy-start.5 = (f32[4,1536]{1,0:T(4,128)S(1)}, f32[4,1536]{1,0:T(4,128)}, u32[]{:S(2)}) copy-start(f32[4,1536]{1,0:T(4,128)} %param.17) | copy-start | bytes 73732
  205.1 45.1 %copy-start.4 = (bf16[3,3,1536]{2,1,0:T(4,128)(2,1)S(1)}, bf16[3,3,1536]{2,1,0:T(4,128)(2,1)}, u32[]{:S(2)}) copy-start(bf16[3,3,1536]{2,1,0:T(4,128)(2,1)} %param.18) | copy-start | bytes 82948
  208.2 44.5 %all-to-all-start.1 = ((bf16[32,2,512]{2,1,0:T(2,128)(2,1)}), bf16[32,2,512]{2,1,0:T(2,128)(2,1)S(1)}, u32[]{:S(2)}, u32[]{:S(2)}) async-start(bf16[32,2,512]{2,1,0:T(2,128)(2,1)} %reshape.339), calls=%async_computation.1 | async-start | bytes 131072 | tf_op jit(solution)/shard_map/all_to_all | solution.py:86
  233.4 745.2 %all-gather.5.cloned.1.call-start = ((), (), s32[]{:S(2)}) async-start(), calls=%async_computation.8 | async-start | bytes 2162688 | tf_op jit(solution)/shard_map/all_gather | solution.py:98
  253.6 966.1 %reduce-scatter.5.cloned.1.call-start = ((), (), s32[]{:S(2)}) async-start(), calls=%async_computation.9 | async-start | bytes 7864320 | tf_op jit(solution)/shard_map/reduce_scatter | solution.py:154
  408.6 3.8 copy-start.2
  969.2 3.6 copy-start.7
  986.8 0.7 copy-start.6
  989.3 54.2 %all-to-all-start.2 = ((s32[32,1,1]{2,1,0:T(1,128)}), s32[32,1,1]{2,1,0:T(1,128)S(1)}, u32[]{:S(2)}, u32[]{:S(2)}) async-start(s32[32,1,1]{2,1,0:T(1,128)} %copy.135), calls=%async_computation.4 | async-start | bytes 32768 | tf_op jit(solution)/shard_map/all_to_all | solution.py:190
  1043.5 149.6 %all-to-all-start.3 = ((bf16[32,128,2,512]{3,1,2,0:T(8,128)(2,1)}), bf16[32,128,2,512]{3,1,2,0:T(8,128)(2,1)}, u32[]{:S(2)}, u32[]{:S(2)}) async-start(bf16[32,128,2,512]{3,1,2,0:T(8,128)(2,1)} %scatter_fusion), calls=%async_computation.5 | async-start | bytes 16777216 | tf_op jit(solution)/shard_map/all_to_all | solution.py:189
  1195.2 24.5 %copy-start.1 = (bf16[1536,512]{1,0:T(8,128)(2,1)S(1)}, bf16[1536,512]{1,0:T(8,128)(2,1)}, u32[]{:S(2)}) copy-start(bf16[1536,512]{1,0:T(8,128)(2,1)} %param.13) | copy-start | bytes 4718596
Sparse Core Ops, SparseCore 0:
  26.2 144.5 all-gather.2
  205.2 164.0 reduce-scatter.2
  371.7 135.9 all-gather.4
  987.0 64.7 reduce-scatter.4
